TPU v7x, 256 devices: a whole 4x4x8 slice. The times are simulated.
256 devices in a mesh: grp: 8 (over y, x_lo), blk: 32 (over z, x_hi, core).
Axes of the slice: x: 4 (x_hi: 2, x_lo: 2; x = x_hi * 2 + x_lo), y: 4, z: 8, core: 2. Of those that a mesh axis runs over, the one named last changes fastest.
Arguments:
- student: bfloat16 [49152, 1024], P(('grp', 'blk')), parts along dimension 0, may hold values from -6 to 6
- teacher: bfloat16 [49152, 1024], P(('grp', 'blk')), parts along dimension 0, may hold values from -6 to 6
Outputs:
- grad_student: float32 [49152, 1024], P(('grp', 'blk')), parts along dimension 0
There are 8 independent parts, one for each index of `grp`. A program takes and returns all parts, laid end to end along the dimension named above; each array names one. Nothing has to cross between parts.
All inputs are finite; a program needn't handle non-finite values.
Results may differ from a plain program's by a relative error of at most 0.01.
Values may be sent and summed in bfloat16 or wider, within the bound.
A program may use at most 128 MiB of HBM per device.

v0:
```python
import jax
import jax.numpy as jnp
from jax import lax
from jax.sharding import PartitionSpec as P

D = 1024


def normalize(values):
    floats = values.astype(jnp.float32)
    norms = jnp.sqrt(jnp.sum(floats * floats, axis=1, keepdims=True) + 1e-06)
    return (floats / norms, norms)


def split_product(left, right):
    left_hi = left.astype(jnp.bfloat16)
    left_lo = (left - left_hi.astype(jnp.float32)).astype(jnp.bfloat16)
    return jnp.dot(left_hi, right, preferred_element_type=jnp.float32) + jnp.dot(
        left_lo, right, preferred_element_type=jnp.float32
    )


def body(student, teacher):
    row_count = student.shape[0]
    text_count = row_count * lax.axis_size("blk")
    s_float, norm_h = normalize(student)
    s_half = s_float.astype(jnp.bfloat16)
    t_float, teacher_norm = normalize(teacher)
    t_half = t_float.astype(jnp.bfloat16)
    s_wide = s_half.astype(jnp.float32)
    s_piece = lax.all_gather(s_half, "blk", axis=0, tiled=True)
    t_piece = lax.all_gather(t_half, "blk", axis=0, tiled=True)
    gram_s = lax.dot_general(
        s_half, s_piece, (((1,), (1,)), ((), ())), preferred_element_type=jnp.float32
    )
    gram_t = lax.dot_general(
        t_half, t_piece, (((1,), (1,)), ((), ())), preferred_element_type=jnp.float32
    )
    product = split_product(gram_s - gram_t, s_piece)
    g_s = product * (D / jnp.sqrt(jnp.float32(text_count)))
    along = jnp.sum(s_wide * g_s, axis=1, keepdims=True)
    return (g_s - s_wide * along) / norm_h


def solution(mesh):
    in_specs = (P(("grp", "blk"), None), P(("grp", "blk"), None))
    out_specs = P(("grp", "blk"), None)
    return jax.shard_map(body, mesh=mesh, in_specs=in_specs, out_specs=out_specs, check_vma=False)
```

profile of v0, /device:TPU:1, one launch (start us, length us, event | category | flops | bytes accessed | tf_op | source)
XLA Modules:
  0.0 279.3 jit_solution(15285107789413137432)
XLA Ops:
  6.5 0.0 all-gather.3.cloned.1.call-start
  6.5 1.2 fusion.6
  7.7 1.9 fusion.7
  9.6 0.0 all-gather.3.cloned.1.call-update
  9.6 0.0 all-gather.5.cloned.1.call-start
  9.7 1.2 fusion.8
  10.8 2.0 fusion.9
  12.8 0.0 all-gather.5.cloned.1.call-update
  12.8 0.0 copy-start
  12.8 118.9 %all-gather.3.cloned.1.call-done = bf16[6144,1024]{1,0:T(8,128)(2,1)} async-done(((bf16[192,1024]{1,0:T(8,128)(2,1)}), bf16[6144,1024]{1,0:T(8,128)(2,1)}) %all-gather.3.cloned.1.call-update) | async-done | bytes 12582928 | tf_op jit(solution)/shard_map/all_gather | solution.py:31
  131.7 11.2 %fusion.13 = f32[192,6144]{1,0:T(8,128)} fusion(bf16[192,1024]{1,0:T(8,128)(2,1)} %fusion.7, bf16[6144,1024]{1,0:T(8,128)(2,1)} %all-gather.3.cloned.1.call-done), kind=kOutput, calls=%fused_computation.23 | convolution fusion | flops 2415919104 | bytes 17694720 | tf_op jit(solution)/shard_map/dot_general | solution.py:33
  142.9 105.9 %all-gather.5.cloned.1.call-done = bf16[6144,1024]{1,0:T(8,128)(2,1)} async-done(((bf16[192,1024]{1,0:T(8,128)(2,1)}), bf16[6144,1024]{1,0:T(8,128)(2,1)}) %all-gather.5.cloned.1.call-update) | async-done | bytes 12582928 | tf_op jit(solution)/shard_map/all_gather | solution.py:32
  248.8 0.0 copy-done
  248.8 10.2 %convolution_subtract_fusion = f32[192,6144]{1,0:T(8,128)S(1)} fusion(f32[192,6144]{1,0:T(8,128)} %fusion.13, bf16[192,1024]{1,0:T(8,128)(2,1)S(1)} %copy-done, bf16[6144,1024]{1,0:T(8,128)(2,1)} %all-gather.5.cloned.1.call-done), kind=kOutput, calls=%fused_computation | convolution fusion | flops 2417098752 | bytes 22413312 | tf_op jit(solution)/shard_map/dot_general | solution.py:36
  259.0 0.0 copy-start.1
  259.0 6.1 %fusion.4 = f32[192,1024]{1,0:T(8,128)S(1)} fusion(bf16[6144,1024]{1,0:T(8,128)(2,1)} %all-gather.3.cloned.1.call-done, f32[192,6144]{1,0:T(8,128)S(1)} %convolution_subtract_fusion), kind=kOutput, calls=%fused_computation.6 | convolution fusion | flops 2417098752 | bytes 18087936 | tf_op jit(solution)/shard_map/dot_general | solution.py:18
  265.1 0.0 copy-done.1
  265.1 0.0 copy-start.2
  265.1 6.2 %fusion.10 = (f32[192]{0:T(256)S(1)}, f32[192,1024]{1,0:T(8,128)S(1)}) fusion(bf16[192,1024]{1,0:T(8,128)(2,1)S(1)} %copy-done.1, f32[192,1024]{1,0:T(8,128)S(1)} %fusion.4, bf16[6144,1024]{1,0:T(8,128)(2,1)} %all-gather.3.cloned.1.call-done, f32[192,6144]{1,0:T(8,128)S(1)} %convolution_subtract_fusion), kind=kOutput, calls=%fused_computation.18 | convolution fusion | flops 2421620480 | bytes 19268352 | tf_op jit(solution)/shard_map/dot_general | solution.py:18
  271.3 0.0 copy-done.2
  271.3 1.1 fusion.12
  (2 shorter events, 0.0 us)
Async XLA Ops:
  6.5 125.2 %all-gather.3.cloned.1.call-start = ((), (), s32[]{:S(2)}) async-start(), calls=%async_computation | async-start | bytes 12976128 | tf_op jit(solution)/shard_map/all_gather | solution.py:31
  9.6 239.2 %all-gather.5.cloned.1.call-start = ((), (), s32[]{:S(2)}) async-start(), calls=%async_computation.1 | async-start | bytes 12976128 | tf_op jit(solution)/shard_map/all_gather | solution.py:32
  12.8 236.0 %copy-start = (bf16[192,1024]{1,0:T(8,128)(2,1)S(1)}, bf16[192,1024]{1,0:T(8,128)(2,1)}, u32[]{:S(2)}) copy-start(bf16[192,1024]{1,0:T(8,128)(2,1)} %fusion.9) | copy-start | bytes 1179652
  259.0 6.1 %copy-start.1 = (bf16[192,1024]{1,0:T(8,128)(2,1)S(1)}, bf16[192,1024]{1,0:T(8,128)(2,1)}, u32[]{:S(2)}) copy-start(bf16[192,1024]{1,0:T(8,128)(2,1)} %fusion.7) | copy-start | bytes 1179652
  265.1 6.2 %copy-start.2 = (bf16[192,1024]{1,0:T(8,128)(2,1)S(1)}, bf16[192,1024]{1,0:T(8,128)(2,1)}, u32[]{:S(2)}) copy-start(bf16[192,1024]{1,0:T(8,128)(2,1)} %param.2) | copy-start | bytes 1179652
Sparse Core Ops, SparseCore 0:
  10.1 121.5 all-gather.2
  134.5 114.2 all-gather.4
where the time goes:
time: 280 us; the launch traced here: 279 us
  waiting for transfers between devices  225 us (80%)
  matrix products  33.6 us (12%)
  between operations  13.5 us (5%)
  other arithmetic  7.27 us (3%)
    all_gather x1, waiting for transfers between devices, body(): s_piece = lax.all_gather(s_half, 'blk', axis=0, tiled=True)  119 us
    all_gather x1, waiting for transfers between devices, body(): t_piece = lax.all_gather(t_half, 'blk', axis=0, tiled=True)  106 us
    dot_general x1, matrix products, body(): lax.dot_general(s_half, s_piece, (((1,), (1,)), ((), ())), preferred_elem...  11.2 us
    dot_general x1, matrix products, body(): lax.dot_general(t_half, t_piece, (((1,), (1,)), ((), ())), preferred_elem...  10.2 us
    dot_general x1, matrix products, split_product(): jnp.dot(left_lo, right, preferred_element_type=jnp.float32)  6.19 us
    dot_general x1, matrix products, split_product(): jnp.dot(left_hi, right, preferred_element_type=jnp.float32)  6.07 us
  transfers between devices with their start and end apart: 2, of which 2 were waited for; matrix products, arithmetic and copies ran while one was open for 5% of the time, Pallas kernels for 0%

commit v1 on v0

v1 whole, which is shorter than its diff:
```python
import functools

import jax
import jax.numpy as jnp
from jax import lax
from jax.experimental import pallas as pl
from jax.experimental.pallas import tpu as pltpu
from jax.sharding import PartitionSpec as P

MESH = pl.DeviceIdType.MESH
D = 1024
RING = 8
HALF = RING // 2
W = D // RING
SUBS = 4
CHUNK = 4 * W + 2 * W + W // 2
SUB = CHUNK // SUBS
BF = jnp.bfloat16
F32 = jnp.float32


def kernel(
    student, teacher, out, s_own, t_own, norm, s_ext, st, tt, own, sendb, recvb, xsend, xrecv, total,
    gath, acc, core_ss, core_rs, rs_ss, rs_rs, x_ss, x_rs, ag_ss, ag_rs, fw_ss, fw_rs,
):
    rows = student.shape[0]
    blk = lax.axis_index("blk")
    z, xh, core = blk // 4, (blk // 2) % 2, blk % 2
    texts = rows * lax.axis_size("blk")
    shift = 2.0 * rows / D

    def at(dz, dx, dc):
        return {"blk": ((z + dz + RING) % RING) * 4 + ((xh + dx) % 2) * 2 + (core + dc) % 2}

    up, down, across, twin = at(1, 0, 0), at(-1, 0, 0), at(0, 1, 0), at(0, 0, 1)
    ring = {1: up, -1: down}
    barrier = pltpu.get_barrier_semaphore()
    for peer in (up, down, across, twin):
        pl.semaphore_signal(barrier, inc=1, device_id=peer, device_id_type=MESH)

    def remote(src, dst, ss, rs, peer):
        return pltpu.make_async_remote_copy(
            src_ref=src, dst_ref=dst, send_sem=ss, recv_sem=rs, device_id=peer, device_id_type=MESH
        )

    x = student[...].astype(F32)
    n = jnp.sqrt(jnp.sum(x * x, axis=1, keepdims=True) + 1e-06)
    norm[...] = jnp.broadcast_to(n, norm.shape)
    s = (x / n).astype(BF)
    s_own[...] = s
    s_ext[0, :, 0:D] = s
    s_ext[0, :, D : D + D // 2] = s[:, 0 : D // 2]
    st[0] = s.T
    y = teacher[...].astype(F32)
    m = jnp.sqrt(jnp.sum(y * y, axis=1, keepdims=True) + 1e-06)
    t = -(y / m).astype(BF)
    t_own[...] = -t
    tt[0] = t.T

    pl.semaphore_wait(barrier, 4)

    pairs = ((s_ext, 0), (st, 1), (tt, 2))
    swaps = [remote(b.at[0], b.at[1], core_ss.at[i], core_rs.at[i], twin) for b, i in pairs]
    for c in swaps:
        c.start()
    for c in swaps:
        c.wait_recv()

    eye = (
        lax.broadcasted_iota(jnp.int32, (W, W), 0) == lax.broadcasted_iota(jnp.int32, (W, W), 1)
    ).astype(F32) * jnp.where(core == 0, shift, 0.0).astype(F32)

    def mul(a, b):
        return jnp.dot(a, b, preferred_element_type=F32)

    def partial(rel):
        j = (z + rel + RING) % RING
        rj = pl.ds(pl.multiple_of(j * W, W), W)
        rh = pl.ds(pl.multiple_of(j * W + core * (W // 2), W // 2), W // 2)
        ct = pl.ds(pl.multiple_of(core * (D // 2), W), D // 2)
        cs = pl.ds(pl.multiple_of((j + 3 * core) * W, W), 2 * W)
        c2 = pl.ds(pl.multiple_of((j + 2) * W, W), W)
        mt = mul(tt[0, rj, :], s_ext[0, :, ct]) + mul(tt[1, rj, :], s_ext[1, :, ct])
        ms = mul(st[0, rj, :], s_ext[0, :, cs]) + mul(st[1, rj, :], s_ext[1, :, cs])
        m2 = mul(st[0, rh, :], s_ext[0, :, c2]) + mul(st[1, rh, :], s_ext[1, :, c2])
        parts = [mt[:, k * W : (k + 1) * W] for k in range(4)]
        parts += [ms[:, :W] - eye, ms[:, W:], m2]
        return parts

    def put(ref, parts, dtype):
        row = 0
        for p in parts:
            ref[row : row + p.shape[0], :] = p.astype(dtype)
            row += p.shape[0]

    def rows_of(u):
        return pl.ds(u * SUB, SUB)

    def lane(d):
        return 0 if d > 0 else 1

    def shares(d, u):
        return (u < SUBS // 2) == (d > 0)

    def rs(d, k, u):
        i = lane(d)
        return remote(
            sendb.at[i, k - 1, rows_of(u)], recvb.at[i, k - 1, rows_of(u)],
            rs_ss.at[i, k - 1, u], rs_rs.at[i, k - 1, u], ring[d],
        )

    far = partial(HALF)
    put(sendb.at[0, 0], far, BF)
    put(sendb.at[1, 0], far, BF)
    for u in range(SUBS):
        for d in (1, -1):
            if shares(d, u):
                rs(d, 1, u).start()
    for k in (2, 3, 4):
        for d in (1, -1):
            put(own.at[lane(d), k - 2], partial(d * (HALF + 1 - k)), F32)
    put(total, partial(0), F32)

    for k in (2, 3, 4):
        order = [(d, u) for u in range(SUBS) for d in (1, -1)]
        if k == 2:
            order = [p for p in order if not shares(*p)] + [p for p in order if shares(*p)]
        for d, u in order:
            i = lane(d)
            v = own[i, k - 2, rows_of(u), :]
            if k > 2 or shares(d, u):
                rs(d, k - 1, u).wait_recv()
                v = v + recvb[i, k - 2, rows_of(u), :].astype(F32)
            sendb[i, k - 1, rows_of(u), :] = v.astype(BF)
            rs(d, k, u).start()

    def xc(u):
        return remote(xsend.at[rows_of(u)], xrecv.at[rows_of(u)], x_ss.at[u], x_rs.at[u], across)

    for u in range(SUBS):
        v = total[rows_of(u), :]
        for d in (1, -1):
            rs(d, 4, u).wait_recv()
            v = v + recvb[lane(d), 3, rows_of(u), :].astype(F32)
        total[rows_of(u), :] = v
        xsend[rows_of(u), :] = v.astype(BF)
        xc(u).start()

    def ag(d, k, u):
        i = lane(d)
        a, b = (-d * (k - 1)) % RING, (-d * k) % RING
        return remote(
            gath.at[core, a, rows_of(u)], gath.at[core, b, rows_of(u)],
            ag_ss.at[i, k - 1, u], ag_rs.at[i, k - 1, u], ring[d],
        )

    def fw(r, u):
        ref = gath.at[core, r % RING, rows_of(u)]
        return remote(ref, ref, fw_ss.at[r % RING, u], fw_rs.at[r % RING, u], twin)

    for u in range(SUBS):
        xc(u).wait_recv()
        v = total[rows_of(u), :] + xrecv[rows_of(u), :].astype(F32)
        gath[core, 0, rows_of(u), :] = v.astype(BF)
        for d in (1, -1):
            ag(d, 1, u).start()
        fw(0, u).start()

    acc[...] = jnp.zeros_like(acc)

    def apply(r):
        r = r % RING
        for u in range(SUBS):
            fw(r, u).wait_recv()
        j = (z + r) % RING

        def block(c, k):
            return gath[c, r, k * W : (k + 1) * W, :]

        mt = jnp.concatenate([block(c, k) for c in (0, 1) for k in range(4)], axis=1)
        b2 = jnp.concatenate([gath[c, r, 6 * W : CHUNK, :] for c in (0, 1)], axis=0)
        ms = jnp.concatenate([block(0, 4), block(0, 5), b2, block(1, 4), block(1, 5)], axis=1)
        tj = t_own[:, pl.ds(pl.multiple_of(j * W, W), W)]
        sj = s_ext[0, :, pl.ds(pl.multiple_of(j * W, W), W)]
        sn = s_ext[0, :, pl.ds(pl.multiple_of((j + 1) * W, W), 3 * W)]
        acc[:, 0:D] += mul(tj, mt)
        wide = pl.ds(pl.multiple_of(j * W, W), 5 * W)
        acc[:, wide] += mul(sj, ms)
        near = pl.ds(pl.multiple_of(j * W, W), W)
        acc[:, near] += lax.dot_general(
            sn, ms[:, W : 4 * W], (((1,), (1,)), ((), ())), preferred_element_type=F32
        )

    for k in (1, 2, 3, 4):
        for u in range(SUBS):
            for d in (1, -1):
                if k < HALF or shares(d, u):
                    ag(d, k, u).wait_recv()
                    if k + 1 < HALF or (k + 1 == HALF and shares(d, u)):
                        ag(d, k + 1, u).start()
                    fw(-d * k, u).start()
        apply(k - 1)
        if k > 1:
            apply(1 - k)
    apply(HALF)

    sw = s_own[...].astype(F32)
    g = acc[:, 0:D] + sw * (shift * (texts // (2 * rows)))
    g = jnp.concatenate([g[:, : D // 2] + acc[:, D:], g[:, D // 2 :]], axis=1)
    g = g * (D / jnp.sqrt(jnp.float32(texts)))
    along = jnp.sum(sw * g, axis=1, keepdims=True)
    out[...] = (g - sw * along) / norm[:, 0:1]

    for c in swaps:
        c.wait_send()
    for u in range(SUBS):
        for d in (1, -1):
            for k in (1, 2, 3, 4):
                if k > 1 or shares(d, u):
                    rs(d, k, u).wait_send()
                if k < HALF or shares(d, u):
                    ag(d, k, u).wait_send()
        xc(u).wait_send()
        for r in range(RING):
            fw(r, u).wait_send()


def body(student, teacher):
    rows = student.shape[0]
    dma = pltpu.SemaphoreType.DMA
    return pl.pallas_call(
        kernel,
        out_shape=jax.ShapeDtypeStruct((rows, D), F32),
        in_specs=[pl.BlockSpec(memory_space=pltpu.VMEM)] * 2,
        out_specs=pl.BlockSpec(memory_space=pltpu.VMEM),
        scratch_shapes=[
            pltpu.VMEM((rows, D), BF),
            pltpu.VMEM((rows, D), BF),
            pltpu.VMEM((rows, 128), F32),
            pltpu.VMEM((2, rows, D + D // 2), BF),
            pltpu.VMEM((2, D, rows), BF),
            pltpu.VMEM((2, D, rows), BF),
            pltpu.VMEM((2, 3, CHUNK, W), F32),
            pltpu.VMEM((2, 4, CHUNK, W), BF),
            pltpu.VMEM((2, 4, CHUNK, W), BF),
            pltpu.VMEM((CHUNK, W), BF),
            pltpu.VMEM((CHUNK, W), BF),
            pltpu.VMEM((CHUNK, W), F32),
            pltpu.VMEM((2, RING, CHUNK, W), BF),
            pltpu.VMEM((rows, D + D // 2), F32),
            dma((3,)), dma((3,)),
            dma((2, 4, SUBS)), dma((2, 4, SUBS)),
            dma((SUBS,)), dma((SUBS,)),
            dma((2, 4, SUBS)), dma((2, 4, SUBS)),
            dma((RING, SUBS)), dma((RING, SUBS)),
        ],
        compiler_params=pltpu.CompilerParams(
            collective_id=0, has_side_effects=True, vmem_limit_bytes=48 * 2**20
        ),
    )(student, teacher)


def solution(mesh):
    in_specs = (P(("grp", "blk"), None), P(("grp", "blk"), None))
    out_specs = P(("grp", "blk"), None)
    return jax.shard_map(body, mesh=mesh, in_specs=in_specs, out_specs=out_specs, check_vma=False)
```

time: 280 us -> 57.9 us (0.21)
  waiting for transfers between devices: 225 us -> 0 us
  Pallas kernels: 0 us -> 54.9 us
  matrix products: 33.6 us -> 0 us
  between operations: 13.5 us -> 0.01 us
  other arithmetic: 7.27 us -> 0 us
  local copies, waits for them, and re-layouts: 0.02 us -> 2.87 us
    all_gather x2 -> x0, waiting for transfers between devices: 225 us -> none  [the longest x1 119 us: body(): s_piece = lax.all_gather(s_half, 'blk', axis=0, tiled=True)]
    pallas_call x0 -> x1, Pallas kernels: none -> 54.9 us  [body(): pl.pallas_call(kernel, out_shape=jax.ShapeDtypeStruct((rows, D), F32), in...]
    dot_general x4 -> x0, matrix products: 33.6 us -> none  [the longest x1 11.2 us: body(): lax.dot_general(s_half, s_piece, (((1,), (1,)), ((), ())), preferred_elem...]
    convert_element_type x2 -> x0, other arithmetic: 3.85 us -> none  [the longest x1 1.95 us: body(): t_half = t_float.astype(jnp.bfloat16)]
    unnamed x6 -> x5, local copies, waits for them, and re-layouts: 0.02 us -> 2.87 us
  transfers between devices with their start and end apart: 2 -> 0, of which waited for: 2 -> 0; matrix products, arithmetic and copies ran while one was open for 5% -> 0% of each run, Pallas kernels for 0% -> 0%
where the time goes in v1:
time: 57.9 us; the launch traced here: 57.8 us
  Pallas kernels  54.9 us (95%)
  local copies, waits for them, and re-layouts  2.87 us (5%)
    pallas_call x1, Pallas kernels, body(): pl.pallas_call(kernel, out_shape=jax.ShapeDtypeStruct((rows, D), F32), in...  54.9 us
    unnamed x5, local copies, waits for them, and re-layouts  2.87 us

profile of v1, /device:TPU:1, one launch (start us, length us, event | category | flops | bytes accessed | tf_op | source)
XLA Modules:
  0.0 57.8 jit_solution(18316281338044984278)
XLA Ops:
  0.0 0.0 copy-start
  0.0 1.0 %copy-done = bf16[192,1024]{1,0:T(8,128)(2,1)S(1)} copy-done((bf16[192,1024]{1,0:T(8,128)(2,1)S(1)}, bf16[192,1024]{1,0:T(8,128)(2,1)}, u32[]{:S(2)}) %copy-start) | copy-done | bytes 393240
  1.0 0.0 copy-start.1
  1.0 1.0 %copy-done.1 = bf16[192,1024]{1,0:T(8,128)(2,1)S(1)} copy-done((bf16[192,1024]{1,0:T(8,128)(2,1)S(1)}, bf16[192,1024]{1,0:T(8,128)(2,1)}, u32[]{:S(2)}) %copy-start.1) | copy-done | bytes 393240
  2.0 54.9 %shard_map.28 = f32[192,1024]{1,0:T(8,128)S(1)} custom-call(bf16[192,1024]{1,0:T(8,128)(2,1)S(1)} %copy-done, bf16[192,1024]{1,0:T(8,128)(2,1)S(1)} %copy-done.1), custom_call_target="tpu_custom_call" | custom-call | tf_op jit(solution)/shard_map/pallas_call | solution.py:231
  56.9 0.9 %copy.4 = f32[192,1024]{1,0:T(8,128)} copy(f32[192,1024]{1,0:T(8,128)S(1)} %shard_map.28) | data formatting | bytes 1572864
Async XLA Ops:
  0.0 1.0 %copy-start = (bf16[192,1024]{1,0:T(8,128)(2,1)S(1)}, bf16[192,1024]{1,0:T(8,128)(2,1)}, u32[]{:S(2)}) copy-start(bf16[192,1024]{1,0:T(8,128)(2,1)} %student.1) | copy-start | bytes 1179652
  1.0 1.0 %copy-start.1 = (bf16[192,1024]{1,0:T(8,128)(2,1)S(1)}, bf16[192,1024]{1,0:T(8,128)(2,1)}, u32[]{:S(2)}) copy-start(bf16[192,1024]{1,0:T(8,128)(2,1)} %teacher.1) | copy-start | bytes 1179652
